TPU v7x, 32 devices: a whole 2x2x4 slice. The times are simulated.
32 devices in a mesh: xy: 8 (over y, x, core), gz: 4 (over z).
Axes of the slice: x: 2, y: 2, z: 4, core: 2. Of those that a mesh axis runs over, the one named last changes fastest.
Arguments:
- velocity: float32 [3, 16, 256, 1024], P(None, 'gz', 'xy'), may hold values from -6 to 6
- magnetic: float32 [3, 8, 128, 512], P(None, 'gz', 'xy'), may hold values from -6 to 6
- slot_block_table: int32 [256], P('xy'), may hold values from 0 to 255, as said below
Outputs:
- updated_fine_velocity: float32 [3, 16, 256, 1024], P(None, 'gz', 'xy')
- magnetic_next: float32 [3, 8, 128, 512], P(None, 'gz', 'xy')
Inputs may be any that keep to these rules, and one draw needn't show every extreme that they name: `slot_block_table`: each block number appears in one slot; the 32 slots of one device along xy hold exactly 4 blocks of every block row.
All inputs are finite; a program needn't handle non-finite values.
Results may differ from a plain program's by a relative error of at most 0.00005.
Values sent between devices are 32-bit elements; how exact they have to be, the bound alone decides.
No kernel may reach another device: no remote copies, remote signals or barrier semaphores. Data moves between devices by JAX's collectives and lax.ppermute only.
A program may use at most 64 MiB of HBM per device.

v0:
```python
import jax
import jax.numpy as jnp
from jax import lax
from jax.sharding import PartitionSpec as P

BLOCK_EDGE = 32


def with_halo(value, sides, width):
    for axis, dim in sides:
        size, length = (lax.axis_size(axis), value.shape[dim])
        up = [(i, (i + 1) % size) for i in range(size)]
        down = [(j, i) for i, j in up]
        last = lax.slice_in_dim(value, length - width, length, axis=dim)
        first = lax.slice_in_dim(value, 0, width, axis=dim)
        before = lax.ppermute(last, axis, up)
        after = lax.ppermute(first, axis, down)
        value = jnp.concatenate([before, value, after], axis=dim)
    return value


def restrict(fine, blk):
    half_width = blk // 2
    s = fine.shape
    v = fine.reshape(s[0], s[1] // 2, 2, s[2], half_width, 2, half_width, 2)
    return (jnp.sum(v, axis=(2, 5, 7)) * 0.125).reshape(
        s[0], s[1] // 2, s[2], half_width * half_width
    )


def inner(padded):
    return padded[:, 1:-1, 1:-1]


def along_z(padded):
    return (padded[:, 2:, 1:-1] - padded[:, :-2, 1:-1]) * 0.5


def along_y(padded):
    return (padded[:, 1:-1, 2:] - padded[:, 1:-1, :-2]) * 0.5


def along_x(padded):
    middle = inner(padded)
    return (jnp.roll(middle, -1, 3) - jnp.roll(middle, 1, 3)) * 0.5


def curl_padded(padded):
    dzv = along_z(padded)
    dyv = along_y(padded)
    dxv = along_x(padded)
    return jnp.stack([dyv[2] - dzv[1], dzv[0] - dxv[2], dxv[1] - dyv[0]])


def cross(a, b):
    return jnp.stack(
        [a[1] * b[2] - a[2] * b[1], a[2] * b[0] - a[0] * b[2], a[0] * b[1] - a[1] * b[0]]
    )


def laplace_padded(padded):
    middle = inner(padded)
    total = padded[:, 2:, 1:-1] + padded[:, :-2, 1:-1] + padded[:, 1:-1, 2:] + padded[:, 1:-1, :-2]
    return total + jnp.roll(middle, 1, 3) + jnp.roll(middle, -1, 3) - 6.0 * middle


def split_into_tiles(magnetic_state, coarse_depth_index, half_width, slot_count):
    return (
        magnetic_state.reshape(
            magnetic_state.shape[0], coarse_depth_index, half_width, slot_count, half_width
        )
        .transpose(0, 1, 3, 2, 4)
        .reshape(magnetic_state.shape[0], coarse_depth_index, slot_count, half_width * half_width)
    )


def assemble_from_tiles(tile_stack, coarse_depth_index, half_width, slot_count):
    return (
        tile_stack.reshape(
            tile_stack.shape[0], coarse_depth_index, slot_count, half_width, half_width
        )
        .transpose(0, 1, 3, 2, 4)
        .reshape(tile_stack.shape[0], coarse_depth_index, half_width, slot_count * half_width)
    )


def body(velocity, magnetic, slot_block_table):
    half_width = BLOCK_EDGE // 2
    slot_count = velocity.shape[2]
    coarse_depth_index = velocity.shape[1] // 2
    column_indices = slot_block_table % slot_count
    sorted_positions = jnp.argsort(slot_block_table)
    dispatched_columns = column_indices[sorted_positions].reshape(1, 1, slot_count, 1)
    ordered = velocity[:, :, sorted_positions]
    got, received_columns = (
        lax.all_to_all(
            restrict(ordered, BLOCK_EDGE), "xy", split_axis=2, concat_axis=2, tiled=True
        ),
        lax.all_to_all(dispatched_columns, "xy", split_axis=2, concat_axis=2, tiled=True),
    )
    column_listing = received_columns.reshape(slot_count)
    grouped_by_column = got[:, :, jnp.argsort(column_listing)]
    coarse_flow_field = assemble_from_tiles(
        grouped_by_column, coarse_depth_index, half_width, slot_count
    )
    emf = cross(coarse_flow_field, magnetic)
    stacked = jnp.concatenate([magnetic, emf], axis=0)
    padded = with_halo(stacked, (("xy", 2), ("gz", 1)), 1)
    field_pad = padded[0:3]
    current = curl_padded(field_pad)
    magnetic_next = magnetic + 0.1 * (curl_padded(padded[3:6]) + 0.5 * laplace_padded(field_pad))
    lorentz_force = cross(current, magnetic)
    returned_back_tiles = split_into_tiles(
        lorentz_force, coarse_depth_index, half_width, slot_count
    )[:, :, column_listing]
    returned = lax.all_to_all(returned_back_tiles, "xy", split_axis=2, concat_axis=2, tiled=True)
    blocks_per_slot = returned[:, :, jnp.argsort(sorted_positions)]
    widened_tiles = jnp.broadcast_to(
        blocks_per_slot.reshape(3, coarse_depth_index, 1, slot_count, half_width, 1, half_width, 1),
        (3, coarse_depth_index, 2, slot_count, half_width, 2, half_width, 2),
    )
    updated_fine_velocity = velocity + 0.1 * widened_tiles.reshape(
        3, coarse_depth_index * 2, slot_count, BLOCK_EDGE * BLOCK_EDGE
    )
    return (updated_fine_velocity, magnetic_next)


def solution(mesh):
    return jax.shard_map(
        body,
        mesh=mesh,
        in_specs=(P(None, "gz", "xy", None), P(None, "gz", "xy", None), P("xy")),
        out_specs=(P(None, "gz", "xy", None), P(None, "gz", "xy", None)),
        check_vma=False,
    )
```

profile of v0, /device:TPU:0, one launch (start us, length us, event | category | flops | bytes accessed | tf_op | source)
XLA Modules:
  0.0 104.9 jit_solution(8437130082161293835)
XLA Ops:
  1.4 2.3 %sort.45 = (s32[32]{0:T(128)}, s32[32]{0:T(128)S(1)}) sort(s32[32]{0:T(128)} %param.5, s32[32]{0:T(128)S(1)} %iota.10), dimensions={0}, to_apply=%region_0.1 | sort | flops 160 | bytes 512 | tf_op jit(solution)/shard_map/jit(argsort)/sort | solution.py:92
  5.7 5.2 %all-to-all-start.1 = ((s32[1,1,32,1]{3,1,0,2:T(1,128)}), s32[1,1,32,1]{3,1,0,2:T(1,128)S(1)}, u32[]{:S(2)}, u32[]{:S(2)}) async-start(s32[1,1,32,1]{3,1,0,2:T(1,128)} %copy.33), calls=%async_computation.1 | async-start | bytes 32768 | tf_op jit(solution)/shard_map/all_to_all | solution.py:99
  10.9 1.5 %fusion.14 = (f32[3,2,16,1]{3,2,1,0:T(8,128)}, f32[3,2,16,1]{3,2,1,0:T(8,128)}) fusion(f32[3,2,16,512]{3,2,1,0:T(8,128)} %param.4), kind=kLoop, calls=%fused_computation.82 | loop fusion | bytes 1536 | tf_op jit(solution)/shard_map/jit(_roll_static)/slice | solution.py:45
  13.6 3.0 %gather_fusion = f32[32,3,4,1024]{3,0,2,1:T(8,128)S(1)} fusion(f32[3,4,32,1024]{3,2,1,0:T(8,128)S(1)} %copy-done, s32[1024]{0:T(1024)} %copy-done.18), kind=kCustom, calls=%fused_computation | custom fusion | bytes 3145856 | tf_op jit(solution)/shard_map/gather | solution.py:94
  16.5 4.0 %copy.43 = f32[3,4,32,1024]{2,3,1,0:T(8,128)} copy(f32[3,4,32,1024]{3,2,1,0:T(8,128)S(1)} %copy-done) | data formatting | bytes 3145728 | tf_op args[0]
  20.5 2.3 %sort.47 = (s32[32]{0:T(128)}, s32[32]{0:T(128)S(1)}) sort(s32[32]{0:T(128)} %copy-done.19, s32[32]{0:T(128)S(1)} %iota.12), dimensions={0}, to_apply=%region_3.4 | sort | flops 160 | bytes 512 | tf_op jit(solution)/shard_map/jit(argsort)/sort | solution.py:117
  23.4 4.0 %copy.31 = f32[3,4,32,1024]{2,3,1,0:T(8,128)} copy(f32[3,4,32,1024]{3,2,1,0:T(8,128)S(1)} %bitcast.34) | data formatting | bytes 3145728 | tf_op jit(solution)/shard_map/gather | solution.py:94
  27.3 7.3 %reduce_sum.9 = f32[3,2,32,16,16]{2,4,3,1,0:T(8,128)S(1)} reduce(f32[3,2,2,32,16,2,16,2]{3,7,6,5,4,2,1,0:T(2,128)} %bitcast.32, f32[]{:T(128)} %constant.10.clone.1), dimensions={2,5,7}, to_apply=%region_1.2 | reduce | flops 344064 | bytes 1769476 | tf_op jit(solution)/shard_map/reduce_sum | solution.py:26
  36.5 4.2 %all-to-all-start = ((f32[3,2,32,256]{3,1,0,2:T(2,128)}), f32[3,2,32,256]{3,1,0,2:T(2,128)S(1)}, u32[]{:S(2)}, u32[]{:S(2)}) async-start(f32[3,2,32,256]{3,1,0,2:T(2,128)} %copy.32), calls=%async_computation | async-start | bytes 393216 | tf_op jit(solution)/shard_map/all_to_all | solution.py:96
  41.4 1.6 %sort.46 = (s32[32]{0:T(128)}, s32[32]{0:T(128)S(1)}) sort(s32[32]{0:T(128)S(1)} %reduce, s32[32]{0:T(128)S(1)} %iota.11), dimensions={0}, to_apply=%region_2.3 | sort | flops 160 | bytes 512 | tf_op jit(solution)/shard_map/jit(argsort)/sort | solution.py:102
  43.0 3.9 %all-to-all-done = f32[3,2,32,256]{3,1,0,2:T(2,128)S(1)} async-done(((f32[3,2,32,256]{3,1,0,2:T(2,128)}), f32[3,2,32,256]{3,1,0,2:T(2,128)S(1)}, u32[]{:S(2)}, u32[]{:S(2)}) %all-to-all-start) | async-done | bytes 196640 | tf_op jit(solution)/shard_map/all_to_all | solution.py:96
  49.8 2.6 %collective-permute-start.1 = (f32[6,2,1,512]{3,2,1,0:T(1,128)S(1)}, f32[6,2,1,512]{3,2,1,0:T(1,128)S(1)}, u32[]{:S(2)}, u32[]{:S(2)}) collective-permute-start(f32[6,2,1,512]{3,2,1,0:T(1,128)S(1)} %get-tuple-element.23), channel_id=1, source_target_pairs={{4,0},{8,4},{12,8},{16,12},{20,16},{24,20},{28,24},{0,28},{5,1},{9... | collective-permute-start | bytes 73736 | tf_op jit(solution)/shard_map/ppermute | solution.py:17
  52.4 1.7 %collective-permute-done = f32[6,2,1,512]{3,2,1,0:T(1,128)S(1)} collective-permute-done((f32[6,2,1,512]{3,2,1,0:T(1,128)S(1)}, f32[6,2,1,512]{3,2,1,0:T(1,128)S(1)}, u32[]{:S(2)}, u32[]{:S(2)}) %collective-permute-start) | collective-permute-done | bytes 24608 | tf_op jit(solution)/shard_map/ppermute | solution.py:16
  54.3 1.6 %collective-permute-start.3 = (f32[6,1,18,512]{3,2,1,0:T(8,128)S(1)}, f32[6,1,18,512]{3,2,1,0:T(8,128)S(1)}, u32[]{:S(2)}, u32[]{:S(2)}) collective-permute-start(f32[6,1,18,512]{3,2,1,0:T(8,128)S(1)} %get-tuple-element.20), channel_id=1, source_target_pairs={{0,1},{1,2},{2,3},{3,0},{4,5},{5,6},{6,7},{7,4},{8,9},{9,10},{10,1... | collective-permute-start | bytes 663560 | tf_op jit(solution)/shard_map/ppermute | solution.py:16
  55.9 2.3 %collective-permute-start.2 = (f32[6,1,18,512]{3,2,1,0:T(8,128)S(1)}, f32[6,1,18,512]{3,2,1,0:T(8,128)S(1)}, u32[]{:S(2)}, u32[]{:S(2)}) collective-permute-start(f32[6,1,18,512]{3,2,1,0:T(8,128)S(1)} %get-tuple-element.21), channel_id=1, source_target_pairs={{1,0},{2,1},{3,2},{0,3},{5,4},{6,5},{7,6},{4,7},{9,8},{10,9},{11,1... | collective-permute-start | bytes 663560 | tf_op jit(solution)/shard_map/ppermute | solution.py:17
  59.0 7.1 %collective-permute-done.3 = f32[6,1,18,512]{3,2,1,0:T(8,128)S(1)} collective-permute-done((f32[6,1,18,512]{3,2,1,0:T(8,128)S(1)}, f32[6,1,18,512]{3,2,1,0:T(8,128)S(1)}, u32[]{:S(2)}, u32[]{:S(2)}) %collective-permute-start.3) | collective-permute-done | bytes 221216 | tf_op jit(solution)/shard_map/ppermute | solution.py:16
  66.0 4.7 %collective-permute-done.2 = f32[6,1,18,512]{3,2,1,0:T(8,128)S(1)} collective-permute-done((f32[6,1,18,512]{3,2,1,0:T(8,128)S(1)}, f32[6,1,18,512]{3,2,1,0:T(8,128)S(1)}, u32[]{:S(2)}, u32[]{:S(2)}) %collective-permute-start.2) | collective-permute-done | bytes 221216 | tf_op jit(solution)/shard_map/ppermute | solution.py:17
  75.3 1.4 %maximum_bitcast_fusion = f32[3,2,32,16,16]{4,2,3,1,0:T(8,128)S(1)} fusion(f32[1,2,16,32,16]{4,3,2,1,0:T(8,128)} %stack.23, f32[1,2,16,32,16]{4,3,2,1,0:T(8,128)} %stack.22, f32[1,2,16,32,16]{4,3,2,1,0:T(8,128)S(1)} %stack.10), kind=kLoop, calls=%fused_computation.5 | loop fusion | flops 98304 | bytes 393216 | tf_op jit(solution)/shard_map/transpose | solution.py:72
  77.5 1.5 %gather_fusion.3 = f32[32,3,2,256]{3,2,1,0:T(2,128)} fusion(f32[3,2,32,256]{3,1,2,0:T(2,128)S(1)} %copy.40, s32[1024]{0:T(1024)S(1)} %pad_clamp_fusion.1), kind=kCustom, calls=%fused_computation.3 | custom fusion | bytes 393344 | tf_op jit(solution)/shard_map/gather | solution.py:113
  78.9 3.4 %all-to-all-start.2 = ((f32[3,2,32,256]{3,1,0,2:T(2,128)}), f32[3,2,32,256]{3,1,0,2:T(2,128)S(1)}, u32[]{:S(2)}, u32[]{:S(2)}) async-start(f32[3,2,32,256]{3,1,0,2:T(2,128)} %bitcast.11), calls=%async_computation.2 | async-start | bytes 393216 | tf_op jit(solution)/shard_map/all_to_all | solution.py:116
  83.5 5.0 %all-to-all-done.2 = f32[3,2,32,256]{3,1,0,2:T(2,128)S(1)} async-done(((f32[3,2,32,256]{3,1,0,2:T(2,128)}), f32[3,2,32,256]{3,1,0,2:T(2,128)S(1)}, u32[]{:S(2)}, u32[]{:S(2)}) %all-to-all-start.2) | async-done | bytes 196640 | tf_op jit(solution)/shard_map/all_to_all | solution.py:116
  89.8 3.2 %broadcast_in_dim.19 = f32[3,2,2,32,16,2,16,2]{3,7,6,5,4,2,1,0:T(2,128)S(1)} broadcast(f32[3,2,32,16,16]{2,4,3,1,0:T(8,128)S(1)} %bitcast.35), dimensions={0,1,3,4,6} | broadcast | bytes 1769472 | tf_op jit(solution)/shard_map/broadcast_in_dim | solution.py:118
  93.0 6.3 %add.55 = f32[3,4,32,1024]{2,3,1,0:T(8,128)} add(f32[3,4,32,1024]{2,3,1,0:T(8,128)} %copy.43, f32[3,4,32,1024]{2,3,1,0:T(8,128)S(1)} %bitcast.33) | non-fusion elementwise | flops 393216 | bytes 4718592 | tf_op jit(solution)/shard_map/add | solution.py:122
  99.3 5.5 %copy.44 = f32[3,4,32,1024]{3,2,1,0:T(8,128)} copy(f32[3,4,32,1024]{2,3,1,0:T(8,128)} %add.55) | data formatting | bytes 3145728
  (95 shorter events, 18.4 us)
Async XLA Ops:
  0.6 12.9 %copy-start = (f32[3,4,32,1024]{3,2,1,0:T(8,128)S(1)}, f32[3,4,32,1024]{3,2,1,0:T(8,128)}, u32[]{:S(2)}) copy-start(f32[3,4,32,1024]{3,2,1,0:T(8,128)} %param.3) | copy-start | bytes 4718596
  4.3 8.1 %copy-start.18 = (s32[1024]{0:T(1024)}, s32[1024]{0:T(1024)S(1)}, u32[]{:S(2)}) copy-start(s32[1024]{0:T(1024)S(1)} %pad_clamp_fusion.3) | copy-start | bytes 12292
  5.7 30.8 %all-to-all-start.1 = ((s32[1,1,32,1]{3,1,0,2:T(1,128)}), s32[1,1,32,1]{3,1,0,2:T(1,128)S(1)}, u32[]{:S(2)}, u32[]{:S(2)}) async-start(s32[1,1,32,1]{3,1,0,2:T(1,128)} %copy.33), calls=%async_computation.1 | async-start | bytes 32768 | tf_op jit(solution)/shard_map/all_to_all | solution.py:99
  13.6 21.2 %copy-start.2 = (f32[3,2,16,511]{3,2,1,0:T(8,128)}, f32[3,2,16,511]{3,2,1,0:T(8,128)S(1)}, u32[]{:S(2)}) copy-start(f32[3,2,16,511]{3,2,1,0:T(8,128)S(1)} %get-tuple-element.37) | copy-start | bytes 588676
  36.5 10.4 %all-to-all-start = ((f32[3,2,32,256]{3,1,0,2:T(2,128)}), f32[3,2,32,256]{3,1,0,2:T(2,128)S(1)}, u32[]{:S(2)}, u32[]{:S(2)}) async-start(f32[3,2,32,256]{3,1,0,2:T(2,128)} %copy.32), calls=%async_computation | async-start | bytes 393216 | tf_op jit(solution)/shard_map/all_to_all | solution.py:96
  48.3 1.3 %copy-start.1 = (f32[3,2,16,512]{3,2,1,0:T(8,128)S(1)}, f32[3,2,16,512]{3,2,1,0:T(8,128)}, u32[]{:S(2)}) copy-start(f32[3,2,16,512]{3,2,1,0:T(8,128)} %param.4) | copy-start | bytes 589828
  49.7 4.4 %collective-permute-start = (f32[6,2,1,512]{3,2,1,0:T(1,128)S(1)}, f32[6,2,1,512]{3,2,1,0:T(1,128)S(1)}, u32[]{:S(2)}, u32[]{:S(2)}) collective-permute-start(f32[6,2,1,512]{3,2,1,0:T(1,128)S(1)} %get-tuple-element.22), channel_id=1, source_target_pairs={{0,4},{4,8},{8,12},{12,16},{16,20},{20,24},{24,28},{28,0},{1,5},{5... | collective-permute-start | bytes 73736 | tf_op jit(solution)/shard_map/ppermute | solution.py:16
  49.8 4.4 %collective-permute-start.1 = (f32[6,2,1,512]{3,2,1,0:T(1,128)S(1)}, f32[6,2,1,512]{3,2,1,0:T(1,128)S(1)}, u32[]{:S(2)}, u32[]{:S(2)}) collective-permute-start(f32[6,2,1,512]{3,2,1,0:T(1,128)S(1)} %get-tuple-element.23), channel_id=1, source_target_pairs={{4,0},{8,4},{12,8},{16,12},{20,16},{24,20},{28,24},{0,28},{5,1},{9... | collective-permute-start | bytes 73736 | tf_op jit(solution)/shard_map/ppermute | solution.py:17
  54.1 18.8 %copy-start.4 = (f32[6,2,1,512]{3,2,1,0:T(1,128)}, f32[6,2,1,512]{3,2,1,0:T(1,128)S(1)}, u32[]{:S(2)}) copy-start(f32[6,2,1,512]{3,2,1,0:T(1,128)S(1)} %collective-permute-done) | copy-start | bytes 73732
  54.1 18.8 %copy-start.6 = (f32[6,2,1,512]{3,2,1,0:T(1,128)}, f32[6,2,1,512]{3,2,1,0:T(1,128)S(1)}, u32[]{:S(2)}) copy-start(f32[6,2,1,512]{3,2,1,0:T(1,128)S(1)} %collective-permute-done.1) | copy-start | bytes 73732
  54.3 11.8 %collective-permute-start.3 = (f32[6,1,18,512]{3,2,1,0:T(8,128)S(1)}, f32[6,1,18,512]{3,2,1,0:T(8,128)S(1)}, u32[]{:S(2)}, u32[]{:S(2)}) collective-permute-start(f32[6,1,18,512]{3,2,1,0:T(8,128)S(1)} %get-tuple-element.20), channel_id=1, source_target_pairs={{0,1},{1,2},{2,3},{3,0},{4,5},{5,6},{6,7},{7,4},{8,9},{9,10},{10,1... | collective-permute-start | bytes 663560 | tf_op jit(solution)/shard_map/ppermute | solution.py:16
  55.9 14.8 %collective-permute-start.2 = (f32[6,1,18,512]{3,2,1,0:T(8,128)S(1)}, f32[6,1,18,512]{3,2,1,0:T(8,128)S(1)}, u32[]{:S(2)}, u32[]{:S(2)}) collective-permute-start(f32[6,1,18,512]{3,2,1,0:T(8,128)S(1)} %get-tuple-element.21), channel_id=1, source_target_pairs={{1,0},{2,1},{3,2},{0,3},{5,4},{6,5},{7,6},{4,7},{9,8},{10,9},{11,1... | collective-permute-start | bytes 663560 | tf_op jit(solution)/shard_map/ppermute | solution.py:17
  77.1 5.2 %copy-start.8 = (f32[3,2,16,511]{3,2,1,0:T(8,128)S(1)}, f32[3,2,16,511]{3,2,1,0:T(8,128)}, u32[]{:S(2)}) copy-start(f32[3,2,16,511]{3,2,1,0:T(8,128)} %get-tuple-element.34) | copy-start | bytes 588676
  77.1 5.2 %copy-start.9 = (f32[3,2,16,511]{3,2,1,0:T(8,128)S(1)}, f32[3,2,16,511]{3,2,1,0:T(8,128)}, u32[]{:S(2)}) copy-start(f32[3,2,16,511]{3,2,1,0:T(8,128)} %get-tuple-element.35) | copy-start | bytes 588676
  77.1 5.2 %copy-start.16 = (f32[3,2,16,1]{3,2,1,0:T(8,128)S(1)}, f32[3,2,16,1]{3,2,1,0:T(8,128)}, u32[]{:S(2)}) copy-start(f32[3,2,16,1]{3,2,1,0:T(8,128)} %get-tuple-element.32) | copy-start | bytes 1156
  77.1 5.2 %copy-start.17 = (f32[3,2,16,1]{3,2,1,0:T(8,128)S(1)}, f32[3,2,16,1]{3,2,1,0:T(8,128)}, u32[]{:S(2)}) copy-start(f32[3,2,16,1]{3,2,1,0:T(8,128)} %get-tuple-element.33) | copy-start | bytes 1156
  77.2 5.4 %copy-start.10 = (f32[3,2,16,512]{3,2,1,0:T(8,128)S(1)}, f32[3,2,16,512]{3,2,1,0:T(8,128)}, u32[]{:S(2)}) copy-start(f32[3,2,16,512]{3,2,1,0:T(8,128)} %fusion.3) | copy-start | bytes 589828
  77.2 5.4 %copy-start.11 = (f32[3,2,16,512]{3,2,1,0:T(8,128)S(1)}, f32[3,2,16,512]{3,2,1,0:T(8,128)}, u32[]{:S(2)}) copy-start(f32[3,2,16,512]{3,2,1,0:T(8,128)} %get-tuple-element.30) | copy-start | bytes 589828
  77.2 5.4 %copy-start.3 = (f32[3,2,16,511]{3,2,1,0:T(8,128)S(1)}, f32[3,2,16,511]{3,2,1,0:T(8,128)}, u32[]{:S(2)}) copy-start(f32[3,2,16,511]{3,2,1,0:T(8,128)} %copy-done.2) | copy-start | bytes 588676
  77.2 5.4 %copy-start.5 = (f32[6,2,1,512]{3,2,1,0:T(1,128)S(1)}, f32[6,2,1,512]{3,2,1,0:T(1,128)}, u32[]{:S(2)}) copy-start(f32[6,2,1,512]{3,2,1,0:T(1,128)} %copy-done.4) | copy-start | bytes 73732
  77.2 5.4 %copy-start.7 = (f32[6,2,1,512]{3,2,1,0:T(1,128)S(1)}, f32[6,2,1,512]{3,2,1,0:T(1,128)}, u32[]{:S(2)}) copy-start(f32[6,2,1,512]{3,2,1,0:T(1,128)} %copy-done.6) | copy-start | bytes 73732
  77.2 5.4 %copy-start.13 = (f32[3,2,16,1]{3,2,1,0:T(8,128)S(1)}, f32[3,2,16,1]{3,2,1,0:T(8,128)}, u32[]{:S(2)}) copy-start(f32[3,2,16,1]{3,2,1,0:T(8,128)} %get-tuple-element.38) | copy-start | bytes 1156
  77.2 5.4 %copy-start.15 = (f32[3,2,16,1]{3,2,1,0:T(8,128)S(1)}, f32[3,2,16,1]{3,2,1,0:T(8,128)}, u32[]{:S(2)}) copy-start(f32[3,2,16,1]{3,2,1,0:T(8,128)} %get-tuple-element.39) | copy-start | bytes 1156
  78.9 9.5 %all-to-all-start.2 = ((f32[3,2,32,256]{3,1,0,2:T(2,128)}), f32[3,2,32,256]{3,1,0,2:T(2,128)S(1)}, u32[]{:S(2)}, u32[]{:S(2)}) async-start(f32[3,2,32,256]{3,1,0,2:T(2,128)} %bitcast.11), calls=%async_computation.2 | async-start | bytes 393216 | tf_op jit(solution)/shard_map/all_to_all | solution.py:116
  (3 other events, 2.2 us)
where the time goes:
time: 106 us; the launch traced here: 105 us
  local copies, waits for them, and re-layouts  35.8 us (34%)
  other arithmetic  26.2 us (25%)
  waiting for transfers between devices  22.3 us (21%)
  starting transfers between devices  19.4 us (18%)
  between operations  1.12 us (1%)
    unnamed x42, local copies, waits for them, and re-layouts  10.9 us
    ppermute x2, waiting for transfers between devices, with_halo(): before = lax.ppermute(last, axis, up)  8.8 us
    reduce_sum x1, other arithmetic, restrict(): jnp.sum(v, axis=(2, 5, 7)) * 0.125  7.27 us
    gather x2, local copies, waits for them, and re-layouts, body(): ordered = velocity[:, :, sorted_positions]  6.93 us
    add x1, other arithmetic, body(): velocity + 0.1 * widened_tiles.reshape(3, coarse_depth_index * 2, slot_co...  6.28 us
    all_to_all x1, starting transfers between devices, body(): lax.all_to_all(dispatched_columns, 'xy', split_axis=2, concat_axis=2, til...  5.2 us
    all_to_all x1, waiting for transfers between devices, body(): lax.all_to_all(returned_back_tiles, 'xy', split_axis=2, concat_axis=2, ti...  4.99 us
    ppermute x2, starting transfers between devices, with_halo(): after = lax.ppermute(first, axis, down)  4.9 us
  transfers between devices with their start and end apart: 7, of which 5 were waited for; matrix products, arithmetic and copies ran while one was open for 28% of the time, Pallas kernels for 0%

commit v1 on v0

--- a/solution.py
+++ b/solution.py
@@ -1,9 +1,44 @@
+import functools
 import jax
 import jax.numpy as jnp
 from jax import lax
 from jax.sharding import PartitionSpec as P
 
 BLOCK_EDGE = 32
+
+
+def wait_face(in_array, dim_k, arr_in):
+    item_now, m_next = (in_array.shape[:dim_k], in_array.shape[dim_k + 1 :])
+    latest = in_array.reshape(*item_now, arr_in, -1, *m_next)
+    return jnp.moveaxis(latest, dim_k, 0)
+
+
+def _serve_points(base_x, which_dim):
+    base_x = jnp.moveaxis(base_x, 0, which_dim)
+    opened = base_x.shape
+    return base_x.reshape(
+        *opened[:which_dim], opened[which_dim] * opened[which_dim + 1], *opened[which_dim + 2 :]
+    )
+
+
+def lay_block(my_data, axis_tag, local_x, q_in):
+    e_next = lax.axis_index(axis_tag)
+    answer = lax.axis_size(axis_tag)
+    carry, s_next = (answer, e_next)
+    state_next = wait_face(my_data, local_x, carry)
+    samples = [state_next[s_next]]
+    at = 1
+    while at < carry:
+        placed = state_next[s_next ^ at]
+        d_next = lax.ppermute(placed, axis_tag, [(jj, jj ^ at) for jj in range(carry)])
+        samples.append(d_next)
+        at += 1
+    local_next = jnp.stack(samples, axis=0)
+    state_next = local_next[s_next ^ jnp.arange(carry)]
+    return _serve_points(state_next, q_in)
+
+
+run_turns_now = functools.partial(lay_block, axis_tag="xy", local_x=2, q_in=2)
 
 
 def with_halo(value, sides, width):
@@ -96,7 +131,7 @@
         lax.all_to_all(
             restrict(ordered, BLOCK_EDGE), "xy", split_axis=2, concat_axis=2, tiled=True
         ),
-        lax.all_to_all(dispatched_columns, "xy", split_axis=2, concat_axis=2, tiled=True),
+        run_turns_now(dispatched_columns),
     )
     column_listing = received_columns.reshape(slot_count)
     grouped_by_column = got[:, :, jnp.argsort(column_listing)]

time: 106 us -> 102 us (0.962)
  local copies, waits for them, and re-layouts: 35.8 us -> 32.3 us
  starting transfers between devices: 19.4 us -> 22.2 us
  other arithmetic: 26.2 us -> 24.3 us
  waiting for transfers between devices: 22.3 us -> 21.1 us
    ppermute x0 -> x7, starting transfers between devices: none -> 8.84 us  [lay_block(): lax.ppermute(placed, axis_tag, [(jj, jj ^ at) for jj in range(carry)])]
    all_to_all x1 -> x0, starting transfers between devices: 5.2 us -> none  [body(): lax.all_to_all(dispatched_columns, 'xy', split_axis=2, concat_axis=2, til...]
    all_to_all x1, waiting for transfers between devices: 3.9 us -> 0.01 us  [body(): lax.all_to_all(restrict(ordered, BLOCK_EDGE), 'xy', split_axis=2, concat_...]
    slice x4, local copies, waits for them, and re-layouts: 4.15 us -> 1.69 us  [along_x(): return (jnp.roll(middle, -1, 3) - jnp.roll(middle, 1, 3)) * 0.5]
    ppermute x0 -> x7, waiting for transfers between devices: none -> 1.64 us  [lay_block(): lax.ppermute(placed, axis_tag, [(jj, jj ^ at) for jj in range(carry)])]
    ppermute x2, waiting for transfers between devices: 4.65 us -> 6.09 us  [with_halo(): after = lax.ppermute(first, axis, down)]
    unnamed x42 -> x38, local copies, waits for them, and re-layouts: 10.9 us -> 9.62 us
  transfers between devices with their start and end apart: 7 -> 13, of which waited for: 5 -> 5; matrix products, arithmetic and copies ran while one was open for 28% -> 25% of each run, Pallas kernels for 0% -> 0%
where the time goes in v1:
time: 102 us; the launch traced here: 101 us
  local copies, waits for them, and re-layouts  32.3 us (32%)
  other arithmetic  24.3 us (24%)
  starting transfers between devices  22.2 us (22%)
  waiting for transfers between devices  21.1 us (21%)
  between operations  1.21 us (1%)
    unnamed x38, local copies, waits for them, and re-layouts  9.62 us
    ppermute x7, starting transfers between devices, lay_block(): lax.ppermute(placed, axis_tag, [(jj, jj ^ at) for jj in range(carry)])  8.84 us
    ppermute x2, waiting for transfers between devices, with_halo(): before = lax.ppermute(last, axis, up)  8.4 us
    reduce_sum x1, other arithmetic, restrict(): jnp.sum(v, axis=(2, 5, 7)) * 0.125  7.27 us
    gather x2, local copies, waits for them, and re-layouts, body(): ordered = velocity[:, :, sorted_positions]  7.18 us
    add x1, other arithmetic, body(): velocity + 0.1 * widened_tiles.reshape(3, coarse_depth_index * 2, slot_co...  6.3 us
    ppermute x2, waiting for transfers between devices, with_halo(): after = lax.ppermute(first, axis, down)  6.09 us
    all_to_all x1, waiting for transfers between devices, body(): lax.all_to_all(returned_back_tiles, 'xy', split_axis=2, concat_axis=2, ti...  4.99 us
  transfers between devices with their start and end apart: 13, of which 5 were waited for; matrix products, arithmetic and copies ran while one was open for 25% of the time, Pallas kernels for 0%

profile of v1, /device:TPU:0, one launch (start us, length us, event | category | flops | bytes accessed | tf_op | source)
XLA Modules:
  0.0 101.1 jit_solution(16201033667573360222)
XLA Ops:
  0.7 2.3 %sort.45 = (s32[32]{0:T(128)}, s32[32]{0:T(128)S(1)}) sort(s32[32]{0:T(128)} %param.5, s32[32]{0:T(128)S(1)} %iota.14), dimensions={0}, to_apply=%region_0.1 | sort | flops 160 | bytes 512 | tf_op jit(solution)/shard_map/jit(argsort)/sort | solution.py:127
  4.4 3.4 %collective-permute-start.6 = (s32[1,1,4,1]{2,3,1,0:T(1,128)S(1)}, s32[1,1,4,1]{2,3,1,0:T(1,128)S(1)}, u32[]{:S(2)}, u32[]{:S(2)}) collective-permute-start(s32[1,1,4,1]{2,3,1,0:T(1,128)S(1)} %get-tuple-element.38), channel_id=1, source_target_pairs={{0,28},{4,24},{8,20},{12,16},{16,12},{20,8},{24,4},{28,0},{1,29},{... | collective-permute-start | bytes 56 | tf_op jit(solution)/shard_map/ppermute | solution.py:33
  11.3 3.2 %gather_fusion = f32[32,3,4,1024]{3,0,2,1:T(8,128)S(1)} fusion(f32[3,4,32,1024]{3,2,1,0:T(8,128)} %param.3, s32[1024]{0:T(1024)S(1)} %pad_clamp_fusion.4), kind=kCustom, calls=%fused_computation | custom fusion | bytes 3145856 | tf_op jit(solution)/shard_map/gather | solution.py:129
  14.4 4.0 %copy.35 = f32[3,4,32,1024]{2,3,1,0:T(8,128)} copy(f32[3,4,32,1024]{3,2,1,0:T(8,128)S(1)} %bitcast.69) | data formatting | bytes 3145728 | tf_op jit(solution)/shard_map/gather | solution.py:129
  18.5 7.3 %reduce_sum.9 = f32[3,2,32,16,16]{2,4,3,1,0:T(8,128)S(1)} reduce(f32[3,2,2,32,16,2,16,2]{3,7,6,5,4,2,1,0:T(2,128)} %bitcast.67, f32[]{:T(128)} %constant.20.clone.1), dimensions={2,5,7}, to_apply=%region_1.2 | reduce | flops 344064 | bytes 1769476 | tf_op jit(solution)/shard_map/reduce_sum | solution.py:61
  26.8 3.4 %all-to-all-start = ((f32[3,2,32,256]{3,1,0,2:T(2,128)}), f32[3,2,32,256]{3,1,0,2:T(2,128)S(1)}, u32[]{:S(2)}, u32[]{:S(2)}) async-start(f32[3,2,32,256]{3,1,0,2:T(2,128)} %copy.36), calls=%async_computation | async-start | bytes 393216 | tf_op jit(solution)/shard_map/all_to_all | solution.py:131
  30.4 4.0 %copy.55 = f32[3,4,32,1024]{2,3,1,0:T(8,128)} copy(f32[3,4,32,1024]{3,2,1,0:T(8,128)S(1)} %copy-done) | data formatting | bytes 3145728 | tf_op args[0]
  34.4 1.6 %sort.47 = (s32[32]{0:T(128)}, s32[32]{0:T(128)S(1)}) sort(s32[32]{0:T(128)S(1)} %get-tuple-element.5, s32[32]{0:T(128)S(1)} %iota.17), dimensions={0}, to_apply=%region_3.4 | sort | flops 160 | bytes 512 | tf_op jit(solution)/shard_map/jit(argsort)/sort | solution.py:152
  36.2 2.0 %collective-permute-start.1 = (s32[1,1,4,1]{2,3,1,0:T(1,128)S(1)}, s32[1,1,4,1]{2,3,1,0:T(1,128)S(1)}, u32[]{:S(2)}, u32[]{:S(2)}) collective-permute-start(s32[1,1,4,1]{2,3,1,0:T(1,128)S(1)} %get-tuple-element.43), channel_id=1, source_target_pairs={{0,8},{4,12},{8,0},{12,4},{16,24},{20,28},{24,16},{28,20},{1,9},{5... | collective-permute-start | bytes 56 | tf_op jit(solution)/shard_map/ppermute | solution.py:33
  38.2 1.6 %collective-permute-done.1 = s32[1,1,4,1]{2,3,1,0:T(1,128)S(1)} collective-permute-done((s32[1,1,4,1]{2,3,1,0:T(1,128)S(1)}, s32[1,1,4,1]{2,3,1,0:T(1,128)S(1)}, u32[]{:S(2)}, u32[]{:S(2)}) %collective-permute-start.1) | collective-permute-done | bytes 48 | tf_op jit(solution)/shard_map/ppermute | solution.py:33
  40.6 1.6 %sort.46 = (s32[32]{0:T(128)}, s32[32]{0:T(128)S(1)}) sort(s32[32]{0:T(128)S(1)} %reshape_reshape_transpose.5, s32[32]{0:T(128)S(1)} %iota.16), dimensions={0}, to_apply=%region_2.3 | sort | flops 160 | bytes 512 | tf_op jit(solution)/shard_map/jit(argsort)/sort | solution.py:137
  45.1 2.6 %collective-permute-start.8 = (f32[6,2,1,512]{3,2,1,0:T(1,128)S(1)}, f32[6,2,1,512]{3,2,1,0:T(1,128)S(1)}, u32[]{:S(2)}, u32[]{:S(2)}) collective-permute-start(f32[6,2,1,512]{3,2,1,0:T(1,128)S(1)} %get-tuple-element.21), channel_id=1, source_target_pairs={{4,0},{8,4},{12,8},{16,12},{20,16},{24,20},{28,24},{0,28},{5,1},{9... | collective-permute-start | bytes 73736 | tf_op jit(solution)/shard_map/ppermute | solution.py:52
  47.7 1.5 %collective-permute-done.7 = f32[6,2,1,512]{3,2,1,0:T(1,128)S(1)} collective-permute-done((f32[6,2,1,512]{3,2,1,0:T(1,128)S(1)}, f32[6,2,1,512]{3,2,1,0:T(1,128)S(1)}, u32[]{:S(2)}, u32[]{:S(2)}) %collective-permute-start.7) | collective-permute-done | bytes 24608 | tf_op jit(solution)/shard_map/ppermute | solution.py:51
  49.4 1.6 %collective-permute-start.10 = (f32[6,1,18,512]{3,2,1,0:T(8,128)S(1)}, f32[6,1,18,512]{3,2,1,0:T(8,128)S(1)}, u32[]{:S(2)}, u32[]{:S(2)}) collective-permute-start(f32[6,1,18,512]{3,2,1,0:T(8,128)S(1)} %get-tuple-element.18), channel_id=1, source_target_pairs={{0,1},{1,2},{2,3},{3,0},{4,5},{5,6},{6,7},{7,4},{8,9},{9,10},{10,1... | collective-permute-start | bytes 663560 | tf_op jit(solution)/shard_map/ppermute | solution.py:51
  51.0 2.3 %collective-permute-start.9 = (f32[6,1,18,512]{3,2,1,0:T(8,128)S(1)}, f32[6,1,18,512]{3,2,1,0:T(8,128)S(1)}, u32[]{:S(2)}, u32[]{:S(2)}) collective-permute-start(f32[6,1,18,512]{3,2,1,0:T(8,128)S(1)} %get-tuple-element.19), channel_id=1, source_target_pairs={{1,0},{2,1},{3,2},{0,3},{5,4},{6,5},{7,6},{4,7},{9,8},{10,9},{11,1... | collective-permute-start | bytes 663560 | tf_op jit(solution)/shard_map/ppermute | solution.py:52
  54.1 6.9 %collective-permute-done.10 = f32[6,1,18,512]{3,2,1,0:T(8,128)S(1)} collective-permute-done((f32[6,1,18,512]{3,2,1,0:T(8,128)S(1)}, f32[6,1,18,512]{3,2,1,0:T(8,128)S(1)}, u32[]{:S(2)}, u32[]{:S(2)}) %collective-permute-start.10) | collective-permute-done | bytes 221216 | tf_op jit(solution)/shard_map/ppermute | solution.py:51
  61.0 6.1 %collective-permute-done.9 = f32[6,1,18,512]{3,2,1,0:T(8,128)S(1)} collective-permute-done((f32[6,1,18,512]{3,2,1,0:T(8,128)S(1)}, f32[6,1,18,512]{3,2,1,0:T(8,128)S(1)}, u32[]{:S(2)}, u32[]{:S(2)}) %collective-permute-start.9) | collective-permute-done | bytes 221216 | tf_op jit(solution)/shard_map/ppermute | solution.py:52
  71.7 1.4 %maximum_bitcast_fusion = f32[3,2,32,16,16]{4,2,3,1,0:T(8,128)S(1)} fusion(f32[1,2,16,32,16]{4,3,2,1,0:T(8,128)} %stack.55, f32[1,2,16,32,16]{4,3,2,1,0:T(8,128)} %stack.54, f32[1,2,16,32,16]{4,3,2,1,0:T(8,128)S(1)} %stack.53), kind=kLoop, calls=%fused_computation.6 | loop fusion | flops 98304 | bytes 393216 | tf_op jit(solution)/shard_map/transpose | solution.py:107
  73.9 1.5 %gather_fusion.4 = f32[32,3,2,256]{3,2,1,0:T(2,128)} fusion(f32[3,2,32,256]{3,1,2,0:T(2,128)S(1)} %copy.52, s32[1024]{0:T(1024)S(1)} %pad_clamp_fusion.1), kind=kCustom, calls=%fused_computation.4 | custom fusion | bytes 393344 | tf_op jit(solution)/shard_map/gather | solution.py:148
  75.3 3.4 %all-to-all-start.1 = ((f32[3,2,32,256]{3,1,0,2:T(2,128)}), f32[3,2,32,256]{3,1,0,2:T(2,128)S(1)}, u32[]{:S(2)}, u32[]{:S(2)}) async-start(f32[3,2,32,256]{3,1,0,2:T(2,128)} %bitcast.33), calls=%async_computation.1 | async-start | bytes 393216 | tf_op jit(solution)/shard_map/all_to_all | solution.py:151
  79.9 5.0 %all-to-all-done.1 = f32[3,2,32,256]{3,1,0,2:T(2,128)S(1)} async-done(((f32[3,2,32,256]{3,1,0,2:T(2,128)}), f32[3,2,32,256]{3,1,0,2:T(2,128)S(1)}, u32[]{:S(2)}, u32[]{:S(2)}) %all-to-all-start.1) | async-done | bytes 196640 | tf_op jit(solution)/shard_map/all_to_all | solution.py:151
  86.1 3.2 %broadcast_in_dim.20 = f32[3,2,2,32,16,2,16,2]{3,7,6,5,4,2,1,0:T(2,128)S(1)} broadcast(f32[3,2,32,16,16]{2,4,3,1,0:T(8,128)S(1)} %bitcast.70), dimensions={0,1,3,4,6} | broadcast | bytes 1769472 | tf_op jit(solution)/shard_map/broadcast_in_dim | solution.py:153
  89.3 6.3 %add.98 = f32[3,4,32,1024]{2,3,1,0:T(8,128)} add(f32[3,4,32,1024]{2,3,1,0:T(8,128)} %copy.55, f32[3,4,32,1024]{2,3,1,0:T(8,128)S(1)} %bitcast.68) | non-fusion elementwise | flops 393216 | bytes 4718592 | tf_op jit(solution)/shard_map/add | solution.py:157
  95.6 5.5 %copy.56 = f32[3,4,32,1024]{3,2,1,0:T(8,128)} copy(f32[3,4,32,1024]{2,3,1,0:T(8,128)} %add.98) | data formatting | bytes 3145728
  (108 shorter events, 18.3 us)
Async XLA Ops:
  4.4 31.8 %collective-permute-start.6 = (s32[1,1,4,1]{2,3,1,0:T(1,128)S(1)}, s32[1,1,4,1]{2,3,1,0:T(1,128)S(1)}, u32[]{:S(2)}, u32[]{:S(2)}) collective-permute-start(s32[1,1,4,1]{2,3,1,0:T(1,128)S(1)} %get-tuple-element.38), channel_id=1, source_target_pairs={{0,28},{4,24},{8,20},{12,16},{16,12},{20,8},{24,4},{28,0},{1,29},{... | collective-permute-start | bytes 56 | tf_op jit(solution)/shard_map/ppermute | solution.py:33
  7.8 30.4 %collective-permute-start.5 = (s32[1,1,4,1]{2,3,1,0:T(1,128)S(1)}, s32[1,1,4,1]{2,3,1,0:T(1,128)S(1)}, u32[]{:S(2)}, u32[]{:S(2)}) collective-permute-start(s32[1,1,4,1]{2,3,1,0:T(1,128)S(1)} %get-tuple-element.39), channel_id=1, source_target_pairs={{0,24},{4,28},{8,16},{12,20},{16,8},{20,12},{24,0},{28,4},{1,25},{... | collective-permute-start | bytes 56 | tf_op jit(solution)/shard_map/ppermute | solution.py:33
  8.5 29.7 %collective-permute-start.4 = (s32[1,1,4,1]{2,3,1,0:T(1,128)S(1)}, s32[1,1,4,1]{2,3,1,0:T(1,128)S(1)}, u32[]{:S(2)}, u32[]{:S(2)}) collective-permute-start(s32[1,1,4,1]{2,3,1,0:T(1,128)S(1)} %get-tuple-element.40), channel_id=1, source_target_pairs={{0,20},{4,16},{8,28},{12,24},{16,4},{20,0},{24,12},{28,8},{1,21},{... | collective-permute-start | bytes 56 | tf_op jit(solution)/shard_map/ppermute | solution.py:33
  9.8 28.4 %collective-permute-start.3 = (s32[1,1,4,1]{2,3,1,0:T(1,128)S(1)}, s32[1,1,4,1]{2,3,1,0:T(1,128)S(1)}, u32[]{:S(2)}, u32[]{:S(2)}) collective-permute-start(s32[1,1,4,1]{2,3,1,0:T(1,128)S(1)} %get-tuple-element.41), channel_id=1, source_target_pairs={{0,16},{4,20},{8,24},{12,28},{16,0},{20,4},{24,8},{28,12},{1,17},{... | collective-permute-start | bytes 56 | tf_op jit(solution)/shard_map/ppermute | solution.py:33
  10.1 28.1 %collective-permute-start.2 = (s32[1,1,4,1]{2,3,1,0:T(1,128)S(1)}, s32[1,1,4,1]{2,3,1,0:T(1,128)S(1)}, u32[]{:S(2)}, u32[]{:S(2)}) collective-permute-start(s32[1,1,4,1]{2,3,1,0:T(1,128)S(1)} %get-tuple-element.42), channel_id=1, source_target_pairs={{0,12},{4,8},{8,4},{12,0},{16,28},{20,24},{24,20},{28,16},{1,13},{... | collective-permute-start | bytes 56 | tf_op jit(solution)/shard_map/ppermute | solution.py:33
  26.8 15.5 %all-to-all-start = ((f32[3,2,32,256]{3,1,0,2:T(2,128)}), f32[3,2,32,256]{3,1,0,2:T(2,128)S(1)}, u32[]{:S(2)}, u32[]{:S(2)}) async-start(f32[3,2,32,256]{3,1,0,2:T(2,128)} %copy.36), calls=%async_computation | async-start | bytes 393216 | tf_op jit(solution)/shard_map/all_to_all | solution.py:131
  30.3 5.8 %copy-start.12 = (f32[3,2,16,1]{3,2,1,0:T(8,128)}, f32[3,2,16,1]{3,2,1,0:T(8,128)S(1)}, u32[]{:S(2)}) copy-start(f32[3,2,16,1]{3,2,1,0:T(8,128)S(1)} %get-tuple-element.36) | copy-start | bytes 1156
  30.3 5.8 %copy-start.14 = (f32[3,2,16,1]{3,2,1,0:T(8,128)}, f32[3,2,16,1]{3,2,1,0:T(8,128)S(1)}, u32[]{:S(2)}) copy-start(f32[3,2,16,1]{3,2,1,0:T(8,128)S(1)} %get-tuple-element.37) | copy-start | bytes 1156
  30.4 5.7 %copy-start.2 = (f32[3,2,16,511]{3,2,1,0:T(8,128)}, f32[3,2,16,511]{3,2,1,0:T(8,128)S(1)}, u32[]{:S(2)}) copy-start(f32[3,2,16,511]{3,2,1,0:T(8,128)S(1)} %get-tuple-element.35) | copy-start | bytes 588676
  36.2 3.6 %collective-permute-start.1 = (s32[1,1,4,1]{2,3,1,0:T(1,128)S(1)}, s32[1,1,4,1]{2,3,1,0:T(1,128)S(1)}, u32[]{:S(2)}, u32[]{:S(2)}) collective-permute-start(s32[1,1,4,1]{2,3,1,0:T(1,128)S(1)} %get-tuple-element.43), channel_id=1, source_target_pairs={{0,8},{4,12},{8,0},{12,4},{16,24},{20,28},{24,16},{28,20},{1,9},{5... | collective-permute-start | bytes 56 | tf_op jit(solution)/shard_map/ppermute | solution.py:33
  38.2 1.7 %collective-permute-start = (s32[1,1,4,1]{2,3,1,0:T(1,128)S(1)}, s32[1,1,4,1]{2,3,1,0:T(1,128)S(1)}, u32[]{:S(2)}, u32[]{:S(2)}) collective-permute-start(s32[1,1,4,1]{2,3,1,0:T(1,128)S(1)} %get-tuple-element.44), channel_id=1, source_target_pairs={{0,4},{4,0},{8,12},{12,8},{16,20},{20,16},{24,28},{28,24},{1,5},{5... | collective-permute-start | bytes 56 | tf_op jit(solution)/shard_map/ppermute | solution.py:33
  45.0 4.2 %collective-permute-start.7 = (f32[6,2,1,512]{3,2,1,0:T(1,128)S(1)}, f32[6,2,1,512]{3,2,1,0:T(1,128)S(1)}, u32[]{:S(2)}, u32[]{:S(2)}) collective-permute-start(f32[6,2,1,512]{3,2,1,0:T(1,128)S(1)} %get-tuple-element.20), channel_id=1, source_target_pairs={{0,4},{4,8},{8,12},{12,16},{16,20},{20,24},{24,28},{28,0},{1,5},{5... | collective-permute-start | bytes 73736 | tf_op jit(solution)/shard_map/ppermute | solution.py:51
  45.1 4.2 %collective-permute-start.8 = (f32[6,2,1,512]{3,2,1,0:T(1,128)S(1)}, f32[6,2,1,512]{3,2,1,0:T(1,128)S(1)}, u32[]{:S(2)}, u32[]{:S(2)}) collective-permute-start(f32[6,2,1,512]{3,2,1,0:T(1,128)S(1)} %get-tuple-element.21), channel_id=1, source_target_pairs={{4,0},{8,4},{12,8},{16,12},{20,16},{24,20},{28,24},{0,28},{5,1},{9... | collective-permute-start | bytes 73736 | tf_op jit(solution)/shard_map/ppermute | solution.py:52
  49.2 20.1 %copy-start.4 = (f32[6,2,1,512]{3,2,1,0:T(1,128)}, f32[6,2,1,512]{3,2,1,0:T(1,128)S(1)}, u32[]{:S(2)}) copy-start(f32[6,2,1,512]{3,2,1,0:T(1,128)S(1)} %collective-permute-done.7) | copy-start | bytes 73732
  49.3 20.1 %copy-start.6 = (f32[6,2,1,512]{3,2,1,0:T(1,128)}, f32[6,2,1,512]{3,2,1,0:T(1,128)S(1)}, u32[]{:S(2)}) copy-start(f32[6,2,1,512]{3,2,1,0:T(1,128)S(1)} %collective-permute-done.8) | copy-start | bytes 73732
  49.4 11.6 %collective-permute-start.10 = (f32[6,1,18,512]{3,2,1,0:T(8,128)S(1)}, f32[6,1,18,512]{3,2,1,0:T(8,128)S(1)}, u32[]{:S(2)}, u32[]{:S(2)}) collective-permute-start(f32[6,1,18,512]{3,2,1,0:T(8,128)S(1)} %get-tuple-element.18), channel_id=1, source_target_pairs={{0,1},{1,2},{2,3},{3,0},{4,5},{5,6},{6,7},{7,4},{8,9},{9,10},{10,1... | collective-permute-start | bytes 663560 | tf_op jit(solution)/shard_map/ppermute | solution.py:51
  51.0 16.1 %collective-permute-start.9 = (f32[6,1,18,512]{3,2,1,0:T(8,128)S(1)}, f32[6,1,18,512]{3,2,1,0:T(8,128)S(1)}, u32[]{:S(2)}, u32[]{:S(2)}) collective-permute-start(f32[6,1,18,512]{3,2,1,0:T(8,128)S(1)} %get-tuple-element.19), channel_id=1, source_target_pairs={{1,0},{2,1},{3,2},{0,3},{5,4},{6,5},{7,6},{4,7},{9,8},{10,9},{11,1... | collective-permute-start | bytes 663560 | tf_op jit(solution)/shard_map/ppermute | solution.py:52
  73.5 5.4 %copy-start.10 = (f32[3,2,16,512]{3,2,1,0:T(8,128)S(1)}, f32[3,2,16,512]{3,2,1,0:T(8,128)}, u32[]{:S(2)}) copy-start(f32[3,2,16,512]{3,2,1,0:T(8,128)} %fusion.3) | copy-start | bytes 589828
  73.6 5.4 %copy-start.3 = (f32[3,2,16,511]{3,2,1,0:T(8,128)S(1)}, f32[3,2,16,511]{3,2,1,0:T(8,128)}, u32[]{:S(2)}) copy-start(f32[3,2,16,511]{3,2,1,0:T(8,128)} %copy-done.2) | copy-start | bytes 588676
  73.6 5.4 %copy-start.5 = (f32[6,2,1,512]{3,2,1,0:T(1,128)S(1)}, f32[6,2,1,512]{3,2,1,0:T(1,128)}, u32[]{:S(2)}) copy-start(f32[6,2,1,512]{3,2,1,0:T(1,128)} %copy-done.4) | copy-start | bytes 73732
  73.6 5.4 %copy-start.7 = (f32[6,2,1,512]{3,2,1,0:T(1,128)S(1)}, f32[6,2,1,512]{3,2,1,0:T(1,128)}, u32[]{:S(2)}) copy-start(f32[6,2,1,512]{3,2,1,0:T(1,128)} %copy-done.6) | copy-start | bytes 73732
  73.6 5.4 %copy-start.13 = (f32[3,2,16,1]{3,2,1,0:T(8,128)S(1)}, f32[3,2,16,1]{3,2,1,0:T(8,128)}, u32[]{:S(2)}) copy-start(f32[3,2,16,1]{3,2,1,0:T(8,128)} %copy-done.12) | copy-start | bytes 1156
  73.6 5.4 %copy-start.15 = (f32[3,2,16,1]{3,2,1,0:T(8,128)S(1)}, f32[3,2,16,1]{3,2,1,0:T(8,128)}, u32[]{:S(2)}) copy-start(f32[3,2,16,1]{3,2,1,0:T(8,128)} %copy-done.14) | copy-start | bytes 1156
  75.3 9.5 %all-to-all-start.1 = ((f32[3,2,32,256]{3,1,0,2:T(2,128)}), f32[3,2,32,256]{3,1,0,2:T(2,128)S(1)}, u32[]{:S(2)}, u32[]{:S(2)}) async-start(f32[3,2,32,256]{3,1,0,2:T(2,128)} %bitcast.33), calls=%async_computation.1 | async-start | bytes 393216 | tf_op jit(solution)/shard_map/all_to_all | solution.py:151
  (7 other events, 35.3 us)
